TPU v7x, 32 devices: a whole 2x2x4 slice. The times are simulated.
32 devices in a mesh: vocab: 4 (over z), expert: 8 (over y, x, core).
Axes of the slice: x: 2, y: 2, z: 4, core: 2. Of those that a mesh axis runs over, the one named last changes fastest.
Arguments:
- token_ids: int32 [1024], replicated, may hold values from 0 to 75967
- word_mask: int32 [75968], P('vocab'), may hold values 0 or 1
- embed_table: bfloat16 [75968, 4096], P('vocab', 'expert'), may hold values from -6 to 6
- attn_out: bfloat16 [1024, 4096], P('expert', 'vocab'), may hold values from -6 to 6
- in_gain: float32 [4096], replicated, may hold values from 0.25 to 1.75
- key_weight: bfloat16 [4096, 512], P(None, 'vocab'), may hold values from -0.09375 to 0.09375
- key_gain: float32 [128], replicated, may hold values from 0.25 to 1.75
- post_gain: float32 [4096], replicated, may hold values from 0.25 to 1.75
- routes: int32 [1024, 8], P('expert'), may hold values from 0 to 15, all different within a row; in each aligned block of 128 rows (0 to 127, 128 to 255, ...) at most 96 rows name the same one
- gate_ints: int32 [1024, 8], P('expert'), may hold values from 1 to 63
- w_gate: bfloat16 [32, 4096, 768], P(('expert', 'vocab')), may hold values from -0.09375 to 0.09375
- w_up: bfloat16 [32, 4096, 768], P(('expert', 'vocab')), may hold values from -0.09375 to 0.09375
- w_down: bfloat16 [32, 768, 4096], P(('expert', 'vocab')), may hold values from -0.15625 to 0.15625
Outputs:
- expert_out: bfloat16 [1024, 4096], P('expert', 'vocab')
- key_heads: bfloat16 [1024, 512], P('expert', 'vocab')
Inputs may be any that keep to these rules, and one draw needn't show every extreme that they name: `routes`: each row names 8 different experts; within the 128 rows of one index of expert no expert is named by more than 96 rows, and in some such blocks one is named by exactly 96.
All inputs are finite; a program needn't handle non-finite values. No bound on the sum of `word_mask` on one device may be relied on, other than what follows from the above.
Results may differ from a plain program's by a relative error of at most 0.008.
Values may be sent and summed in bfloat16 or wider, within the bound.
A program may use at most 192 MiB of HBM per device.

v0:
```python
import jax
import jax.numpy as jnp
from jax import lax
from jax.sharding import PartitionSpec as P


def rms_rows(values, scale_gain):
    inverse_rms = lax.rsqrt(jnp.mean(values * values, axis=-1, keepdims=True) + 1e-06)
    return values * inverse_rms * scale_gain


def on_device(
    token_ids,
    word_mask,
    embed_table,
    attn_out,
    in_gain,
    key_weight,
    key_gain,
    post_gain,
    routes,
    gate_ints,
    w_gate,
    w_up,
    w_down,
):
    n_vocab = lax.axis_size("vocab")
    n_expert = lax.axis_size("expert")
    vocab_rows = embed_table.shape[0]
    experts_total = n_expert * n_vocab // 2
    whole_mesh = ("expert", "vocab")
    my_vocab = lax.axis_index("vocab")
    my_expert = (lax.axis_index("expert") * n_vocab + my_vocab) // 2
    gate_share = gate_ints.astype(jnp.float32) / jnp.sum(gate_ints, axis=1, keepdims=True).astype(
        jnp.float32
    )
    onehot = routes[:, :, None] == jnp.arange(experts_total, dtype=jnp.int32)[None, None, :]
    share_of = jnp.sum(jnp.where(onehot, gate_share[:, :, None], 0.0), axis=1)
    all_shares = lax.all_gather(share_of, "expert", axis=0, tiled=True)
    my_share = lax.dynamic_slice_in_dim(all_shares, my_expert, 1, axis=1)
    own_rows = attn_out.shape[0] // n_vocab
    attn_full = lax.all_gather(attn_out, "vocab", axis=1, tiled=True)
    attn_rows = lax.dynamic_slice_in_dim(attn_full, my_vocab * own_rows, own_rows, axis=0)
    local_ids = token_ids - my_vocab * vocab_rows
    inside = (local_ids >= 0) & (local_ids < vocab_rows)
    safe_ids = jnp.clip(local_ids, 0, vocab_rows - 1)
    keep_row = inside & (word_mask[safe_ids] == 1)
    partial_value = jnp.where(
        keep_row[:, None], embed_table[safe_ids], jnp.zeros_like(embed_table[:1])
    )
    moved_rows = lax.all_to_all(partial_value, "expert", split_axis=0, concat_axis=1, tiled=True)
    rows = lax.psum_scatter(moved_rows, "vocab", scatter_dimension=0, tiled=True)
    rows = rows.astype(jnp.float32)
    mid_rows = (rows + attn_rows.astype(jnp.float32)).astype(jnp.bfloat16)
    expert_in = rms_rows(mid_rows.astype(jnp.float32), post_gain).astype(jnp.bfloat16)
    tokens_in = lax.all_gather(expert_in, whole_mesh, axis=0, tiled=True)
    normed_rows = rms_rows(rows, in_gain).astype(jnp.bfloat16)
    tokens_in, normed_rows = lax.optimization_barrier((tokens_in, normed_rows))
    key_rows = lax.all_gather(normed_rows, "vocab", axis=0, tiled=True)
    gate_val = jnp.dot(tokens_in, w_gate[0], preferred_element_type=jnp.float32)
    up_val = jnp.dot(tokens_in, w_up[0], preferred_element_type=jnp.float32)
    hidden = (jax.nn.silu(gate_val) * up_val).astype(jnp.bfloat16)
    parts = jnp.dot(hidden, w_down[0], preferred_element_type=jnp.float32)
    weighted = (parts * my_share).astype(jnp.bfloat16)
    weighted, key_rows = lax.optimization_barrier((weighted, key_rows))
    raw_keys = jnp.dot(key_rows, key_weight, preferred_element_type=jnp.float32)
    key_heads = rms_rows(raw_keys, key_gain).astype(jnp.bfloat16)
    by_tokens = lax.psum_scatter(weighted, "expert", scatter_dimension=0, tiled=True)
    expert_out = lax.psum_scatter(by_tokens, "vocab", scatter_dimension=1, tiled=True)
    return (expert_out, key_heads)


def solution(mesh):
    return jax.shard_map(
        on_device,
        mesh=mesh,
        in_specs=(
            P(),
            P("vocab"),
            P("vocab", "expert"),
            P("expert", "vocab"),
            P(),
            P(None, "vocab"),
            P(),
            P(),
            P("expert", None),
            P("expert", None),
            P(("expert", "vocab"), None, None),
            P(("expert", "vocab"), None, None),
            P(("expert", "vocab"), None, None),
        ),
        out_specs=(P("expert", "vocab"), P("expert", "vocab")),
        check_vma=False,
    )
```

profile of v0, /device:TPU:0, one launch (start us, length us, event | category | flops | bytes accessed | tf_op | source)
XLA Modules:
  0.0 295.7 jit_solution(1607068945751043418)
XLA Ops:
  7.2 0.0 copy-start
  7.2 0.0 all-gather.4.cloned.1.call-start
  7.2 0.7 all-gather.4.cloned.1.call-update
  7.9 0.0 reduce-scatter.4.cloned.1.call-start
  8.0 0.7 fusion.14
  8.7 0.0 copy-start.5
  8.7 5.9 %gather_fusion = s32[1024]{0:T(1024)S(1)} fusion(s32[18992]{0:T(1024)} %param.14, s32[1024]{0:T(1024)S(1)} %fusion.14), kind=kCustom, calls=%fused_computation | custom fusion | bytes 12288 | tf_op jit(solution)/shard_map/gather | solution.py:47
  14.6 13.3 %gather_fusion.1 = bf16[1024,512]{1,0:T(8,128)(2,1)S(1)} fusion(bf16[18992,512]{1,0:T(8,128)(2,1)} %param.15, s32[1024]{0:T(1024)S(1)} %fusion.14), kind=kCustom, calls=%fused_computation.1 | custom fusion | bytes 2101248 | tf_op jit(solution)/shard_map/gather | solution.py:49
  27.9 0.0 copy-done.5
  27.9 0.0 copy-start.2
  27.9 0.0 copy-start.3
  27.9 0.0 copy-start.4
  28.0 0.0 copy-start.6
  28.0 0.2 broadcast_select_fusion
  28.2 20.3 %all_to_all.16 = bf16[8,128,512]{2,1,0:T(8,128)(2,1)S(1)} all-to-all(bf16[8,128,512]{2,1,0:T(8,128)(2,1)S(1)} %broadcast_select_fusion), channel_id=1, replica_groups=mesh['vocab'=4,'expert'=8] {'expert'}, dimensions={0} | all-to-all | bytes 2097152 | tf_op jit(solution)/shard_map/all_to_all | solution.py:51
  48.5 1.1 copy.25
  49.6 0.0 reduce-scatter.4.cloned.1.call-update
  49.7 0.0 all-gather.6.cloned.1.call-start
  49.7 0.0 all-gather.4.cloned.1.call-done
  49.7 26.6 %reduce-scatter.4.cloned.1.call-done = bf16[32,4096]{1,0:T(8,128)(2,1)} async-done(((bf16[128,4096]{1,0:T(8,128)(2,1)}), bf16[32,4096]{1,0:T(8,128)(2,1)}) %reduce-scatter.4.cloned.1.call-update) | async-done | bytes 262160 | tf_op jit(solution)/shard_map/reduce_scatter | solution.py:52
  76.3 1.3 fusion.11
  77.6 0.0 copy-done.2
  77.6 0.0 copy-done.3
  77.6 2.0 fusion.13
  79.6 0.0 all-gather.6.cloned.1.call-update
  79.7 0.0 all-gather.8.cloned.1.call-start
  79.7 0.0 copy-done.4
  79.8 0.0 copy-done.6
  79.8 9.0 %all_gather.14 = f32[1024,16]{0,1:T(8,128)S(1)} all-gather(f32[128,16]{0,1:T(8,128)S(1)} %select_reduce_fusion), channel_id=1, replica_groups=mesh['vocab'=4,'expert'=8] {'expert'}, dimensions={0}, use_global_device_ids=true | all-gather | bytes 73728 | tf_op jit(solution)/shard_map/all_gather | solution.py:39
  88.9 67.0 %all-gather.6.cloned.1.call-done = bf16[1024,4096]{1,0:T(8,128)(2,1)} async-done(((bf16[32,4096]{1,0:T(8,128)(2,1)}), bf16[1024,4096]{1,0:T(8,128)(2,1)}) %all-gather.6.cloned.1.call-update) | async-done | bytes 8388624 | tf_op jit(solution)/shard_map/all_gather | solution.py:56
  155.9 0.0 all-gather.8.cloned.1.call-update
  155.9 0.2 reduce-scatter.6.cloned.1.call-start
  156.1 0.0 copy-start.8
  156.1 0.0 slice-start
  156.2 11.0 %fusion.1 = f32[1024,768]{1,0:T(8,128)S(1)} fusion(bf16[1024,4096]{1,0:T(8,128)(2,1)} %all-gather.6.cloned.1.call-done, bf16[1,4096,768]{2,1,0:T(8,128)(2,1)} %param.24), kind=kOutput, calls=%fused_computation.4 | convolution fusion | flops 6442450944 | bytes 17825792 | tf_op jit(solution)/shard_map/dot_general | solution.py:61
  167.2 0.0 copy-done.8
  167.2 0.0 slice-start.1
  167.2 10.0 %multiply_convert_fusion.1 = bf16[1024,768]{1,0:T(8,128)(2,1)S(1)} fusion(f32[1024,768]{1,0:T(8,128)S(1)} %fusion.1, bf16[1024,4096]{1,0:T(8,128)(2,1)S(1)} %copy-done.8, bf16[1,4096,768]{2,1,0:T(8,128)(2,1)} %param.23), kind=kOutput, calls=%fused_computation.8 | convolution fusion | flops 6447169536 | bytes 19398656 | tf_op jit(solution)/shard_map/dot_general | solution.py:60
  177.2 0.0 slice-done
  177.2 0.0 slice-done.1
  177.2 8.9 %multiply_convert_fusion = bf16[1024,4096]{1,0:T(8,128)(2,1)} fusion(f32[1024]{0:T(1024)S(1)} %bitcast.26, bf16[1024,768]{1,0:T(8,128)(2,1)S(1)} %multiply_convert_fusion.1, bf16[1,768,4096]{2,1,0:T(8,128)(2,1)S(1)} %bitcast.28), kind=kOutput, calls=%fused_computation.2 | convolution fusion | flops 6450839552 | bytes 16257024 | tf_op jit(solution)/shard_map/dot_general | solution.py:63
  186.1 0.0 copy-start.7
  186.1 0.0 all-gather.8.cloned.1.call-done
  186.1 0.0 copy-start.1
  186.1 0.0 reduce-scatter.6.cloned.1.call-update
  186.1 0.0 reduce-scatter.8.cloned.1.call-start
  186.2 72.9 %reduce-scatter.6.cloned.1.call-done = bf16[128,4096]{1,0:T(8,128)(2,1)} async-done(((bf16[1024,4096]{1,0:T(8,128)(2,1)}), bf16[128,4096]{1,0:T(8,128)(2,1)}) %reduce-scatter.6.cloned.1.call-update) | async-done | bytes 1048592 | tf_op jit(solution)/shard_map/reduce_scatter | solution.py:68
  259.0 0.0 reduce-scatter.8.cloned.1.call-update
  259.0 0.0 copy-done
  259.1 0.0 copy-done.1
  259.1 0.6 multiply_reduce_fusion
  259.6 0.0 copy-done.7
  259.6 0.1 multiply_convert_fusion.2
  259.7 0.7 copy.24
  260.5 28.4 %reduce-scatter.8.cloned.1.call-done = bf16[128,1024]{1,0:T(8,128)(2,1)} async-done(((bf16[128,4096]{1,0:T(8,128)(2,1)}), bf16[128,1024]{1,0:T(8,128)(2,1)}) %reduce-scatter.8.cloned.1.call-update) | async-done | bytes 262160 | tf_op jit(solution)/shard_map/reduce_scatter | solution.py:69
  (9 shorter events, 0.1 us)
Async XLA Ops:
  7.2 251.9 %copy-start = (bf16[4096,128]{1,0:T(8,128)(2,1)S(1)}, bf16[4096,128]{1,0:T(8,128)(2,1)}, u32[]{:S(2)}) copy-start(bf16[4096,128]{1,0:T(8,128)(2,1)} %param.18) | copy-start | bytes 3145732
  7.2 42.6 %all-gather.4.cloned.1.call-start = ((), (), s32[]{:S(2)}) async-start(), calls=%async_computation.5 | async-start | bytes 1310720 | tf_op jit(solution)/shard_map/all_gather | solution.py:42
  7.9 68.4 %reduce-scatter.4.cloned.1.call-start = ((), (), s32[]{:S(2)}) async-start(), calls=%async_computation.4 | async-start | bytes 1310720 | tf_op jit(solution)/shard_map/reduce_scatter | solution.py:52
  8.7 19.2 %copy-start.5 = (s32[1024]{0:T(1024)S(1)}, s32[1024]{0:T(1024)}, u32[]{:S(2)}) copy-start(s32[1024]{0:T(1024)} %param.13) | copy-start | bytes 12292
  27.9 49.7 %copy-start.2 = (f32[4096]{0:T(1024)S(1)}, f32[4096]{0:T(1024)}, u32[]{:S(2)}) copy-start(f32[4096]{0:T(1024)} %param.17) | copy-start | bytes 49156
  27.9 49.7 %copy-start.3 = (f32[4096]{0:T(1024)S(1)}, f32[4096]{0:T(1024)}, u32[]{:S(2)}) copy-start(f32[4096]{0:T(1024)} %param.20) | copy-start | bytes 49156
  27.9 51.8 %copy-start.4 = (s32[128,8]{0,1:T(8,128)S(1)}, s32[128,8]{0,1:T(8,128)}, u32[]{:S(2)}) copy-start(s32[128,8]{0,1:T(8,128)} %param.22) | copy-start | bytes 12292
  28.0 51.8 %copy-start.6 = (s32[128,8]{0,1:T(8,128)S(1)}, s32[128,8]{0,1:T(8,128)}, u32[]{:S(2)}) copy-start(s32[128,8]{0,1:T(8,128)} %param.21) | copy-start | bytes 12292
  49.7 106.2 %all-gather.6.cloned.1.call-start = ((), (), s32[]{:S(2)}) async-start(), calls=%async_computation.6 | async-start | bytes 8650752 | tf_op jit(solution)/shard_map/all_gather | solution.py:56
  79.7 106.4 %all-gather.8.cloned.1.call-start = ((), (), s32[]{:S(2)}) async-start(), calls=%async_computation.7 | async-start | bytes 1310720 | tf_op jit(solution)/shard_map/all_gather | solution.py:59
  155.9 103.1 %reduce-scatter.6.cloned.1.call-start = ((), (), s32[]{:S(2)}) async-start(), calls=%async_computation.8 | async-start | bytes 9437184 | tf_op jit(solution)/shard_map/reduce_scatter | solution.py:68
  156.1 11.1 %copy-start.8 = (bf16[1024,4096]{1,0:T(8,128)(2,1)S(1)}, bf16[1024,4096]{1,0:T(8,128)(2,1)}, u32[]{:S(2)}) copy-start(bf16[1024,4096]{1,0:T(8,128)(2,1)} %all-gather.6.cloned.1.call-done) | copy-start | bytes 25165828
  156.1 21.0 %slice-start = ((s8[6291456]{0:T(1024)(128)(4,1)}), s8[4194304]{0:T(1024)(128)(4,1)S(1)}, s32[]{:S(2)}) async-start(s8[6291456]{0:T(1024)(128)(4,1)} %bitcast.27), calls=%async_computation.10 | async-start | bytes 8388608
  167.2 10.0 %slice-start.1 = ((s8[6291456]{0:T(1024)(128)(4,1)}), s8[2097152]{0:T(1024)(128)(4,1)S(1)}, s32[]{:S(2)}) async-start(s8[6291456]{0:T(1024)(128)(4,1)} %bitcast.27), calls=%async_computation.11 | async-start | bytes 4194304
  186.1 73.5 %copy-start.7 = (f32[128]{0:T(128)S(1)}, f32[128]{0:T(128)}, u32[]{:S(2)}) copy-start(f32[128]{0:T(128)} %param.19) | copy-start | bytes 1540
  186.1 73.0 %copy-start.1 = (bf16[128,4096]{1,0:T(8,128)(2,1)S(1)}, bf16[128,4096]{1,0:T(8,128)(2,1)}, u32[]{:S(2)}) copy-start(bf16[128,4096]{1,0:T(8,128)(2,1)} %all-gather.8.cloned.1.call-done) | copy-start | bytes 3145732
  186.1 102.8 %reduce-scatter.8.cloned.1.call-start = ((), (), s32[]{:S(2)}) async-start(), calls=%async_computation.9 | async-start | bytes 1310720 | tf_op jit(solution)/shard_map/reduce_scatter | solution.py:69
Sparse Core Ops, SparseCore 0:
  9.6 30.6 all-gather.3
  49.8 26.4 reduce-scatter.3
  79.8 76.0 all-gather.5
  158.0 26.5 all-gather.7
  188.2 70.7 reduce-scatter.5
  261.7 27.1 reduce-scatter.7
where the time goes:
time: 296 us
  waiting for transfers between devices  196 us (66%)
  matrix products  30.4 us (10%)
  blocking collectives  29.4 us (10%)
  local copies, waits for them, and re-layouts  21.1 us (7%)
  between operations  14.4 us (5%)
  other arithmetic  4.34 us (1%)
    reduce_scatter x1, waiting for transfers between devices, on_device(): lax.psum_scatter(weighted, 'expert', scatter_dimension=0, tiled=True)  72.9 us
    all_gather x1, waiting for transfers between devices, on_device(): tokens_in = lax.all_gather(expert_in, whole_mesh, axis=0, tiled=True)  67 us
    reduce_scatter x1, waiting for transfers between devices, on_device(): lax.psum_scatter(by_tokens, 'vocab', scatter_dimension=1, tiled=True)  28.4 us
    reduce_scatter x1, waiting for transfers between devices, on_device(): lax.psum_scatter(moved_rows, 'vocab', scatter_dimension=0, tiled=True)  26.6 us
    all_to_all x1, blocking collectives, on_device(): lax.all_to_all(partial_value, 'expert', split_axis=0, concat_axis=1, tile...  20.3 us
    gather x1, local copies, waits for them, and re-layouts, on_device(): embed_table[safe_ids]  13.3 us
    dot_general x1, matrix products, on_device(): up_val = jnp.dot(tokens_in, w_up[0], preferred_element_type=jnp.float32)  11 us
    dot_general x1, matrix products, on_device(): gate_val = jnp.dot(tokens_in, w_gate[0], preferred_element_type=jnp.float32)  9.95 us
  transfers between devices with their start and end apart: 6, of which 4 were waited for; matrix products, arithmetic and copies ran while one was open for 18% of the time, Pallas kernels for 0%

commit v1 on v0

--- a/solution.py
+++ b/solution.py
@@ -2,6 +2,17 @@
 import jax.numpy as jnp
 from jax import lax
 from jax.sharding import PartitionSpec as P
+from jax.lax import axis_index, axis_size, ppermute
+
+
+def _bind_slots(q_in):
+    nd = axis_size("expert")
+    lanes = [q_in]
+    for ix in [*range(nd - 1)]:
+        lanes.append(ppermute(lanes[-1], "expert", [(b, (b + 1) % nd) for b in range(nd)]))
+    return jnp.roll(
+        jnp.concatenate(lanes[::-1], axis=0), (axis_index("expert") + 1) * q_in.shape[0], axis=0
+    )
 
 
 def rms_rows(values, scale_gain):
@@ -36,7 +47,7 @@
     )
     onehot = routes[:, :, None] == jnp.arange(experts_total, dtype=jnp.int32)[None, None, :]
     share_of = jnp.sum(jnp.where(onehot, gate_share[:, :, None], 0.0), axis=1)
-    all_shares = lax.all_gather(share_of, "expert", axis=0, tiled=True)
+    all_shares = _bind_slots(share_of)
     my_share = lax.dynamic_slice_in_dim(all_shares, my_expert, 1, axis=1)
     own_rows = attn_out.shape[0] // n_vocab
     attn_full = lax.all_gather(attn_out, "vocab", axis=1, tiled=True)

time: 296 us -> 296 us (level)
  blocking collectives: 29.4 us -> 20.3 us
  waiting for transfers between devices: 196 us -> 204 us
    ppermute x0 -> x7, waiting for transfers between devices: none -> 27.9 us  [_bind_slots(): ppermute(lanes[-1], 'expert', [(b, (b + 1) % nd) for b in range(nd)])]
    all_gather x1, waiting for transfers between devices: 67 us -> 47.8 us  [on_device(): tokens_in = lax.all_gather(expert_in, whole_mesh, axis=0, tiled=True)]
    all_gather x1 -> x0, blocking collectives: 9.05 us -> none  [on_device(): all_shares = lax.all_gather(share_of, 'expert', axis=0, tiled=True)]
  transfers between devices with their start and end apart: 6 -> 13, of which waited for: 4 -> 11; matrix products, arithmetic and copies ran while one was open for 18% -> 18% of each run, Pallas kernels for 0% -> 0%
where the time goes in v1:
time: 296 us
  waiting for transfers between devices  204 us (69%)
  matrix products  30.6 us (10%)
  local copies, waits for them, and re-layouts  21.3 us (7%)
  blocking collectives  20.3 us (7%)
  between operations  14.5 us (5%)
  other arithmetic  4.34 us (1%)
    reduce_scatter x1, waiting for transfers between devices, on_device(): lax.psum_scatter(weighted, 'expert', scatter_dimension=0, tiled=True)  72.7 us
    all_gather x1, waiting for transfers between devices, on_device(): tokens_in = lax.all_gather(expert_in, whole_mesh, axis=0, tiled=True)  47.8 us
    reduce_scatter x1, waiting for transfers between devices, on_device(): lax.psum_scatter(by_tokens, 'vocab', scatter_dimension=1, tiled=True)  28.4 us
    ppermute x7, waiting for transfers between devices, _bind_slots(): ppermute(lanes[-1], 'expert', [(b, (b + 1) % nd) for b in range(nd)])  27.9 us
    reduce_scatter x1, waiting for transfers between devices, on_device(): lax.psum_scatter(moved_rows, 'vocab', scatter_dimension=0, tiled=True)  26.6 us
    all_to_all x1, blocking collectives, on_device(): lax.all_to_all(partial_value, 'expert', split_axis=0, concat_axis=1, tile...  20.3 us
    gather x1, local copies, waits for them, and re-layouts, on_device(): embed_table[safe_ids]  13.3 us
    dot_general x1, matrix products, on_device(): up_val = jnp.dot(tokens_in, w_up[0], preferred_element_type=jnp.float32)  11 us
  transfers between devices with their start and end apart: 13, of which 11 were waited for; matrix products, arithmetic and copies ran while one was open for 18% of the time, Pallas kernels for 0%

profile of v1, /device:TPU:0, one launch (start us, length us, event | category | flops | bytes accessed | tf_op | source)
XLA Modules:
  0.0 295.7 jit_solution(14161803342738990744)
XLA Ops:
  7.2 0.0 copy-start
  7.2 0.0 all-gather.4.cloned.1.call-start
  7.2 0.7 all-gather.4.cloned.1.call-update
  7.9 0.0 reduce-scatter.4.cloned.1.call-start
  8.0 0.7 fusion.17
  8.7 5.9 %gather_fusion = s32[1024]{0:T(1024)S(1)} fusion(s32[18992]{0:T(1024)} %param.14, s32[1024]{0:T(1024)S(1)} %fusion.17), kind=kCustom, calls=%fused_computation | custom fusion | bytes 12288 | tf_op jit(solution)/shard_map/gather | solution.py:58
  14.6 13.3 %gather_fusion.1 = bf16[1024,512]{1,0:T(8,128)(2,1)S(1)} fusion(bf16[18992,512]{1,0:T(8,128)(2,1)} %param.15, s32[1024]{0:T(1024)S(1)} %fusion.17), kind=kCustom, calls=%fused_computation.1 | custom fusion | bytes 2101248 | tf_op jit(solution)/shard_map/gather | solution.py:60
  27.9 0.0 copy-done.5
  27.9 0.0 copy-start.2
  27.9 0.0 copy-start.3
  27.9 0.0 copy-start.4
  28.0 0.0 copy-start.6
  28.0 0.2 broadcast_select_fusion
  28.2 20.3 %all_to_all.16 = bf16[8,128,512]{2,1,0:T(8,128)(2,1)S(1)} all-to-all(bf16[8,128,512]{2,1,0:T(8,128)(2,1)S(1)} %broadcast_select_fusion), channel_id=1, replica_groups=mesh['vocab'=4,'expert'=8] {'expert'}, dimensions={0} | all-to-all | bytes 2097152 | tf_op jit(solution)/shard_map/all_to_all | solution.py:62
  48.5 1.1 copy.25
  49.6 0.0 reduce-scatter.4.cloned.1.call-update
  49.7 0.0 all-gather.6.cloned.1.call-start
  49.7 0.0 all-gather.4.cloned.1.call-done
  49.7 26.6 %reduce-scatter.4.cloned.1.call-done = bf16[32,4096]{1,0:T(8,128)(2,1)} async-done(((bf16[128,4096]{1,0:T(8,128)(2,1)}), bf16[32,4096]{1,0:T(8,128)(2,1)}) %reduce-scatter.4.cloned.1.call-update) | async-done | bytes 262160 | tf_op jit(solution)/shard_map/reduce_scatter | solution.py:63
  76.3 1.3 fusion.14
  77.6 0.0 copy-done.2
  77.6 0.0 copy-done.3
  77.6 2.0 fusion.16
  79.6 0.0 all-gather.6.cloned.1.call-update
  79.7 0.0 all-gather.8.cloned.1.call-start
  79.7 0.0 copy-done.4
  79.8 0.0 copy-done.6
  79.8 0.1 collective-permute-start
  79.9 4.0 %collective-permute-done = f32[128,16]{0,1:T(8,128)S(1)} collective-permute-done((f32[128,16]{0,1:T(8,128)S(1)}, f32[128,16]{0,1:T(8,128)S(1)}, u32[]{:S(2)}, u32[]{:S(2)}) %collective-permute-start) | collective-permute-done | bytes 8224 | tf_op jit(solution)/shard_map/ppermute | solution.py:12
  83.8 0.0 collective-permute-start.1
  83.8 4.0 %collective-permute-done.1 = f32[128,16]{0,1:T(8,128)S(1)} collective-permute-done((f32[128,16]{0,1:T(8,128)S(1)}, f32[128,16]{0,1:T(8,128)S(1)}, u32[]{:S(2)}, u32[]{:S(2)}) %collective-permute-start.1) | collective-permute-done | bytes 8224 | tf_op jit(solution)/shard_map/ppermute | solution.py:12
  87.8 0.0 collective-permute-start.2
  87.8 4.0 %collective-permute-done.2 = f32[128,16]{0,1:T(8,128)S(1)} collective-permute-done((f32[128,16]{0,1:T(8,128)S(1)}, f32[128,16]{0,1:T(8,128)S(1)}, u32[]{:S(2)}, u32[]{:S(2)}) %collective-permute-start.2) | collective-permute-done | bytes 8224 | tf_op jit(solution)/shard_map/ppermute | solution.py:12
  91.8 0.0 collective-permute-start.3
  91.8 4.0 %collective-permute-done.3 = f32[128,16]{0,1:T(8,128)S(1)} collective-permute-done((f32[128,16]{0,1:T(8,128)S(1)}, f32[128,16]{0,1:T(8,128)S(1)}, u32[]{:S(2)}, u32[]{:S(2)}) %collective-permute-start.3) | collective-permute-done | bytes 8224 | tf_op jit(solution)/shard_map/ppermute | solution.py:12
  95.8 0.0 collective-permute-start.4
  95.8 4.0 %collective-permute-done.4 = f32[128,16]{0,1:T(8,128)S(1)} collective-permute-done((f32[128,16]{0,1:T(8,128)S(1)}, f32[128,16]{0,1:T(8,128)S(1)}, u32[]{:S(2)}, u32[]{:S(2)}) %collective-permute-start.4) | collective-permute-done | bytes 8224 | tf_op jit(solution)/shard_map/ppermute | solution.py:12
  99.8 0.0 collective-permute-start.5
  99.8 4.0 %collective-permute-done.5 = f32[128,16]{0,1:T(8,128)S(1)} collective-permute-done((f32[128,16]{0,1:T(8,128)S(1)}, f32[128,16]{0,1:T(8,128)S(1)}, u32[]{:S(2)}, u32[]{:S(2)}) %collective-permute-start.5) | collective-permute-done | bytes 8224 | tf_op jit(solution)/shard_map/ppermute | solution.py:12
  103.7 0.0 collective-permute-start.6
  103.7 4.1 %collective-permute-done.6 = f32[128,16]{0,1:T(8,128)S(1)} collective-permute-done((f32[128,16]{0,1:T(8,128)S(1)}, f32[128,16]{0,1:T(8,128)S(1)}, u32[]{:S(2)}, u32[]{:S(2)}) %collective-permute-start.6) | collective-permute-done | bytes 8224 | tf_op jit(solution)/shard_map/ppermute | solution.py:12
  108.0 0.1 dynamic_slice.9
  108.0 47.8 %all-gather.6.cloned.1.call-done = bf16[1024,4096]{1,0:T(8,128)(2,1)} async-done(((bf16[32,4096]{1,0:T(8,128)(2,1)}), bf16[1024,4096]{1,0:T(8,128)(2,1)}) %all-gather.6.cloned.1.call-update) | async-done | bytes 8388624 | tf_op jit(solution)/shard_map/all_gather | solution.py:67
  155.9 0.0 all-gather.8.cloned.1.call-update
  155.9 0.2 reduce-scatter.6.cloned.1.call-start
  156.1 0.0 copy-start.8
  156.1 0.0 slice-start
  156.1 11.0 %fusion.4 = f32[1024,768]{1,0:T(8,128)S(1)} fusion(bf16[1024,4096]{1,0:T(8,128)(2,1)} %all-gather.6.cloned.1.call-done, bf16[1,4096,768]{2,1,0:T(8,128)(2,1)} %param.24), kind=kOutput, calls=%fused_computation.5 | convolution fusion | flops 6442450944 | bytes 17825792 | tf_op jit(solution)/shard_map/dot_general | solution.py:72
  167.2 0.0 copy-done.8
  167.2 0.0 slice-start.1
  167.2 9.9 %multiply_convert_fusion.1 = bf16[1024,768]{1,0:T(8,128)(2,1)S(1)} fusion(f32[1024,768]{1,0:T(8,128)S(1)} %fusion.4, bf16[1024,4096]{1,0:T(8,128)(2,1)S(1)} %copy-done.8, bf16[1,4096,768]{2,1,0:T(8,128)(2,1)} %param.23), kind=kOutput, calls=%fused_computation.9 | convolution fusion | flops 6447169536 | bytes 19398656 | tf_op jit(solution)/shard_map/dot_general | solution.py:71
  177.2 0.0 slice-done
  177.2 0.0 slice-done.1
  177.2 9.0 %multiply_convert_fusion = bf16[1024,4096]{1,0:T(8,128)(2,1)} fusion(f32[1024]{0:T(1024)S(1)} %bitcast.28, bf16[1024,768]{1,0:T(8,128)(2,1)S(1)} %multiply_convert_fusion.1, bf16[1,768,4096]{2,1,0:T(8,128)(2,1)S(1)} %bitcast.30), kind=kOutput, calls=%fused_computation.2 | convolution fusion | flops 6450839552 | bytes 16257024 | tf_op jit(solution)/shard_map/dot_general | solution.py:74
  186.2 0.0 reduce-scatter.6.cloned.1.call-update
  186.2 0.0 reduce-scatter.8.cloned.1.call-start
  186.3 72.7 %reduce-scatter.6.cloned.1.call-done = bf16[128,4096]{1,0:T(8,128)(2,1)} async-done(((bf16[1024,4096]{1,0:T(8,128)(2,1)}), bf16[128,4096]{1,0:T(8,128)(2,1)}) %reduce-scatter.6.cloned.1.call-update) | async-done | bytes 1048592 | tf_op jit(solution)/shard_map/reduce_scatter | solution.py:79
  259.0 0.0 reduce-scatter.8.cloned.1.call-update
  259.0 0.0 copy-done
  259.0 0.0 copy-done.1
  259.0 0.6 multiply_reduce_fusion
  259.6 0.1 multiply_convert_fusion.2
  259.7 0.7 copy.24
  260.4 28.4 %reduce-scatter.8.cloned.1.call-done = bf16[128,1024]{1,0:T(8,128)(2,1)} async-done(((bf16[128,4096]{1,0:T(8,128)(2,1)}), bf16[128,1024]{1,0:T(8,128)(2,1)}) %reduce-scatter.8.cloned.1.call-update) | async-done | bytes 262160 | tf_op jit(solution)/shard_map/reduce_scatter | solution.py:80
  (29 shorter events, 0.1 us)
Async XLA Ops:
  7.2 251.9 %copy-start = (bf16[4096,128]{1,0:T(8,128)(2,1)S(1)}, bf16[4096,128]{1,0:T(8,128)(2,1)}, u32[]{:S(2)}) copy-start(bf16[4096,128]{1,0:T(8,128)(2,1)} %param.18) | copy-start | bytes 3145732
  7.2 42.6 %all-gather.4.cloned.1.call-start = ((), (), s32[]{:S(2)}) async-start(), calls=%async_computation.5 | async-start | bytes 1310720 | tf_op jit(solution)/shard_map/all_gather | solution.py:53
  7.9 68.4 %reduce-scatter.4.cloned.1.call-start = ((), (), s32[]{:S(2)}) async-start(), calls=%async_computation.4 | async-start | bytes 1310720 | tf_op jit(solution)/shard_map/reduce_scatter | solution.py:63
  8.7 19.2 %copy-start.5 = (s32[1024]{0:T(1024)S(1)}, s32[1024]{0:T(1024)}, u32[]{:S(2)}) copy-start(s32[1024]{0:T(1024)} %param.13) | copy-start | bytes 12292
  27.9 49.7 %copy-start.2 = (f32[4096]{0:T(1024)S(1)}, f32[4096]{0:T(1024)}, u32[]{:S(2)}) copy-start(f32[4096]{0:T(1024)} %param.17) | copy-start | bytes 49156
  27.9 49.7 %copy-start.3 = (f32[4096]{0:T(1024)S(1)}, f32[4096]{0:T(1024)}, u32[]{:S(2)}) copy-start(f32[4096]{0:T(1024)} %param.20) | copy-start | bytes 49156
  27.9 51.8 %copy-start.4 = (s32[128,8]{0,1:T(8,128)S(1)}, s32[128,8]{0,1:T(8,128)}, u32[]{:S(2)}) copy-start(s32[128,8]{0,1:T(8,128)} %param.22) | copy-start | bytes 12292
  28.0 51.8 %copy-start.6 = (s32[128,8]{0,1:T(8,128)S(1)}, s32[128,8]{0,1:T(8,128)}, u32[]{:S(2)}) copy-start(s32[128,8]{0,1:T(8,128)} %param.21) | copy-start | bytes 12292
  49.7 106.2 %all-gather.6.cloned.1.call-start = ((), (), s32[]{:S(2)}) async-start(), calls=%async_computation.6 | async-start | bytes 8650752 | tf_op jit(solution)/shard_map/all_gather | solution.py:67
  79.7 106.6 %all-gather.8.cloned.1.call-start = ((), (), s32[]{:S(2)}) async-start(), calls=%async_computation.7 | async-start | bytes 1310720 | tf_op jit(solution)/shard_map/all_gather | solution.py:70
  79.8 4.0 %collective-permute-start = (f32[128,16]{0,1:T(8,128)S(1)}, f32[128,16]{0,1:T(8,128)S(1)}, u32[]{:S(2)}, u32[]{:S(2)}) collective-permute-start(f32[128,16]{0,1:T(8,128)S(1)} %select_reduce_fusion), channel_id=1, source_target_pairs={{0,1},{1,2},{2,3},{3,4},{4,5},{5,6},{6,7},{7,0},{8,9},{9,10},{10,1... | collective-permute-start | bytes 24584 | tf_op jit(solution)/shard_map/ppermute | solution.py:12
  83.8 4.0 %collective-permute-start.1 = (f32[128,16]{0,1:T(8,128)S(1)}, f32[128,16]{0,1:T(8,128)S(1)}, u32[]{:S(2)}, u32[]{:S(2)}) collective-permute-start(f32[128,16]{0,1:T(8,128)S(1)} %collective-permute-done), channel_id=1, source_target_pairs={{0,1},{1,2},{2,3},{3,4},{4,5},{5,6},{6,7},{7,0},{8,9},{9,10},{10,1... | collective-permute-start | bytes 24584 | tf_op jit(solution)/shard_map/ppermute | solution.py:12
  87.8 4.0 %collective-permute-start.2 = (f32[128,16]{0,1:T(8,128)S(1)}, f32[128,16]{0,1:T(8,128)S(1)}, u32[]{:S(2)}, u32[]{:S(2)}) collective-permute-start(f32[128,16]{0,1:T(8,128)S(1)} %collective-permute-done.1), channel_id=1, source_target_pairs={{0,1},{1,2},{2,3},{3,4},{4,5},{5,6},{6,7},{7,0},{8,9},{9,10},{10,1... | collective-permute-start | bytes 24584 | tf_op jit(solution)/shard_map/ppermute | solution.py:12
  91.8 4.0 %collective-permute-start.3 = (f32[128,16]{0,1:T(8,128)S(1)}, f32[128,16]{0,1:T(8,128)S(1)}, u32[]{:S(2)}, u32[]{:S(2)}) collective-permute-start(f32[128,16]{0,1:T(8,128)S(1)} %collective-permute-done.2), channel_id=1, source_target_pairs={{0,1},{1,2},{2,3},{3,4},{4,5},{5,6},{6,7},{7,0},{8,9},{9,10},{10,1... | collective-permute-start | bytes 24584 | tf_op jit(solution)/shard_map/ppermute | solution.py:12
  95.8 4.0 %collective-permute-start.4 = (f32[128,16]{0,1:T(8,128)S(1)}, f32[128,16]{0,1:T(8,128)S(1)}, u32[]{:S(2)}, u32[]{:S(2)}) collective-permute-start(f32[128,16]{0,1:T(8,128)S(1)} %collective-permute-done.3), channel_id=1, source_target_pairs={{0,1},{1,2},{2,3},{3,4},{4,5},{5,6},{6,7},{7,0},{8,9},{9,10},{10,1... | collective-permute-start | bytes 24584 | tf_op jit(solution)/shard_map/ppermute | solution.py:12
  99.8 4.0 %collective-permute-start.5 = (f32[128,16]{0,1:T(8,128)S(1)}, f32[128,16]{0,1:T(8,128)S(1)}, u32[]{:S(2)}, u32[]{:S(2)}) collective-permute-start(f32[128,16]{0,1:T(8,128)S(1)} %collective-permute-done.4), channel_id=1, source_target_pairs={{0,1},{1,2},{2,3},{3,4},{4,5},{5,6},{6,7},{7,0},{8,9},{9,10},{10,1... | collective-permute-start | bytes 24584 | tf_op jit(solution)/shard_map/ppermute | solution.py:12
  103.7 4.1 %collective-permute-start.6 = (f32[128,16]{0,1:T(8,128)S(1)}, f32[128,16]{0,1:T(8,128)S(1)}, u32[]{:S(2)}, u32[]{:S(2)}) collective-permute-start(f32[128,16]{0,1:T(8,128)S(1)} %collective-permute-done.5), channel_id=1, source_target_pairs={{0,1},{1,2},{2,3},{3,4},{4,5},{5,6},{6,7},{7,0},{8,9},{9,10},{10,1... | collective-permute-start | bytes 24584 | tf_op jit(solution)/shard_map/ppermute | solution.py:12
  155.9 103.1 %reduce-scatter.6.cloned.1.call-start = ((), (), s32[]{:S(2)}) async-start(), calls=%async_computation.8 | async-start | bytes 9437184 | tf_op jit(solution)/shard_map/reduce_scatter | solution.py:79
  156.1 11.1 %copy-start.8 = (bf16[1024,4096]{1,0:T(8,128)(2,1)S(1)}, bf16[1024,4096]{1,0:T(8,128)(2,1)}, u32[]{:S(2)}) copy-start(bf16[1024,4096]{1,0:T(8,128)(2,1)} %all-gather.6.cloned.1.call-done) | copy-start | bytes 25165828
  156.1 21.0 %slice-start = ((s8[6291456]{0:T(1024)(128)(4,1)}), s8[4194304]{0:T(1024)(128)(4,1)S(1)}, s32[]{:S(2)}) async-start(s8[6291456]{0:T(1024)(128)(4,1)} %bitcast.29), calls=%async_computation.10 | async-start | bytes 8388608
  167.2 10.0 %slice-start.1 = ((s8[6291456]{0:T(1024)(128)(4,1)}), s8[2097152]{0:T(1024)(128)(4,1)S(1)}, s32[]{:S(2)}) async-start(s8[6291456]{0:T(1024)(128)(4,1)} %bitcast.29), calls=%async_computation.11 | async-start | bytes 4194304
  186.2 73.4 %copy-start.7 = (f32[128]{0:T(128)S(1)}, f32[128]{0:T(128)}, u32[]{:S(2)}) copy-start(f32[128]{0:T(128)} %param.19) | copy-start | bytes 1540
  186.2 72.8 %copy-start.1 = (bf16[128,4096]{1,0:T(8,128)(2,1)S(1)}, bf16[128,4096]{1,0:T(8,128)(2,1)}, u32[]{:S(2)}) copy-start(bf16[128,4096]{1,0:T(8,128)(2,1)} %all-gather.8.cloned.1.call-done) | copy-start | bytes 3145732
  186.2 102.6 %reduce-scatter.8.cloned.1.call-start = ((), (), s32[]{:S(2)}) async-start(), calls=%async_computation.9 | async-start | bytes 1310720 | tf_op jit(solution)/shard_map/reduce_scatter | solution.py:80
Sparse Core Ops, SparseCore 0:
  9.6 30.6 all-gather.3
  49.8 26.4 reduce-scatter.3
  79.8 76.0 all-gather.5
  157.9 26.5 all-gather.7
  188.2 70.7 reduce-scatter.5
  261.7 27.1 reduce-scatter.7
